TPU v7x, 32 devices: a whole 2x2x4 slice. The times are simulated.
32 devices in a mesh: groups: 2 (over y), sub: 4 (over z), rhs: 2 (over x), face: 2 (over core).
Axes of the slice: x: 2, y: 2, z: 4, core: 2. Of those that a mesh axis runs over, the one named last changes fastest.
Arguments:
- mortar_in: bfloat16 [1024, 64, 256], P(('groups', 'sub'), 'rhs'), parts along dimension 0, may hold values from -6 to 6
- pump_rate: float32 [128], P(('groups', 'rhs')), parts along dimension 0, may hold values from 4 to 16
- well_cell: int32 [128], P(('groups', 'rhs')), parts along dimension 0, may hold values from 0 to 131071
- face_owner: int32 [2048, 1], P(('groups', 'sub', 'face')), parts along dimension 0, may hold values from 0 to 3; in each aligned block of 128 rows (0 to 127, 128 to 255, ...) at most 64 rows name the same one
- face_slot: int32 [2048], P(('groups', 'sub', 'face')), parts along dimension 0, may hold values from 0 to 127
- face_scale: bfloat16 [2048, 256], P(('groups', 'sub', 'face')), parts along dimension 0, may hold values from 0.5 to 2
- section: int32 [8], P(('groups', 'sub')), parts along dimension 0, may hold values 0 or 1
- basis: bfloat16 [8, 256, 256], P(('groups', 'sub')), parts along dimension 0, may hold values from -0.375 to 0.375
- projection: bfloat16 [256, 256], replicated, may hold values from -0.375 to 0.375
Outputs:
- result: float32 [1024, 64, 256], P(('groups', 'sub', 'face'), 'rhs'), parts along dimension 0
There are 2 independent parts, one for each index of `groups`. A program takes and returns all parts, laid end to end along the dimension named above; an argument that names none is the same for every part. Nothing has to cross between parts.
Inputs may be any that keep to these rules, and one draw needn't show every extreme that they name: `face_owner`: among the 128 faces of one device no subdomain is named by more than 64 faces, a bound that some block reaches.
All inputs are finite; a program needn't handle non-finite values. No bound on the sum of `section` on one device may be relied on, other than what follows from the above.
Results may differ from a plain program's by a relative error of at most 0.004.
Values may be sent and summed in bfloat16 or wider, within the bound.
A program may use at most 64 MiB of HBM per device.

v0:
```python
import functools

import jax
import jax.numpy as jnp
from jax import lax
from jax.experimental import pallas as pl
from jax.experimental.pallas import tpu as pltpu
from jax.sharding import PartitionSpec as P

MESH = pl.DeviceIdType.MESH
F32, BF16 = jnp.float32, jnp.bfloat16


def row_to_column(row, length):
    rows = lax.broadcasted_iota(jnp.int32, (length, length), 0)
    lanes = lax.broadcasted_iota(jnp.int32, (length, length), 1)
    spread = jnp.broadcast_to(row, (length, length))
    return jnp.sum(jnp.where(rows == lanes, spread, 0.0), axis=1, keepdims=True)


def kernel(
    sizes,
    owner_hbm, slot_hbm, section_hbm, cell_hbm, rate_hbm, mortar_ref, scale_ref, basis_ref,
    projection_ref,
    total, projection_out,
    owner_ref, slot_ref, section_ref, cell_ref, rate_ref,
    code_ref, gathered, codes, pumped, weights,
    local_sems, own_send, swap_send, swap_recv,
    z_send, z_recv, x_send, x_recv, core_send, core_recv,
):
    subs, width, faces, blocks, cols, dofs = sizes
    me_z, me_x, me_f = lax.axis_index("sub"), lax.axis_index("rhs"), lax.axis_index("face")
    half = blocks // 2
    share = faces // width
    other_f = 1 - me_f

    low = 1 - (2 * me_z) // subs
    margin = low * me_z + (1 - low) * (subs - 1 - me_z)

    def source(k):
        beyond = (k - 2 * margin - 1 + 4 * subs) // (4 * subs)
        side = (1 - beyond) * (2 * (k % 2) - 1) + beyond * (2 * low - 1)
        reach = (1 - beyond) * ((k + 1) // 2) + beyond * (k - margin)
        return me_z + side * reach, me_z - side

    def inside(z):
        return jnp.logical_and(z >= 0, z < subs)

    def part(z, x, f, kind):
        if kind == 2:
            return codes.at[z, f]
        at = pl.ds(pl.multiple_of(f * faces + x * share, share), share)
        return gathered.at[z, kind, at, :]

    def remote(src, dst, send, recv, device):
        return pltpu.make_async_remote_copy(
            src_ref=src, dst_ref=dst, send_sem=send, recv_sem=recv,
            device_id=device, device_id_type=MESH,
        )

    barrier = pltpu.get_barrier_semaphore()
    pl.semaphore_signal(barrier, inc=1, device_id={"face": other_f}, device_id_type=MESH)
    for z in (me_z - 1, me_z + 1):
        @pl.when(inside(z))
        def _():
            pl.semaphore_signal(barrier, inc=1, device_id={"sub": z}, device_id_type=MESH)
    for dx in range(1, width):
        pl.semaphore_signal(
            barrier, inc=1, device_id={"rhs": lax.rem(me_x + dx, width)}, device_id_type=MESH
        )
    load_scale = pltpu.make_async_copy(
        scale_ref, gathered.at[me_z, 0, pl.ds(pl.multiple_of(me_f * faces, faces), faces), :],
        local_sems.at[0],
    )
    load_basis = pltpu.make_async_copy(basis_ref.at[0], gathered.at[me_z, 1], local_sems.at[1])
    load_mortar = pltpu.make_async_copy(
        mortar_ref.at[pl.ds(me_f * half, half)], pumped, local_sems.at[2]
    )
    small = [
        pltpu.make_async_copy(src, dst, local_sems.at[4 + i])
        for i, (src, dst) in enumerate((
            (owner_hbm, owner_ref), (slot_hbm, slot_ref), (section_hbm, section_ref),
            (cell_hbm, cell_ref), (rate_hbm, rate_ref),
        ))
    ]
    load_projection = pltpu.make_async_copy(projection_ref, projection_out, local_sems.at[3])
    load_scale.start()
    load_basis.start()
    for copy in small:
        copy.start()
    load_mortar.start()
    load_projection.start()

    for copy in small:
        copy.wait()
    code_ref[...] = (owner_ref[...] * blocks + slot_ref[...]) * 2 + jnp.broadcast_to(
        section_ref[...], owner_ref.shape
    )
    codes[me_z, me_f] = code_ref[...]
    load_scale.wait()
    load_basis.wait()
    neighbours = (me_z + subs - 1) // subs + (2 * subs - 2 - me_z) // subs
    pl.semaphore_wait(barrier, width + neighbours)

    sends = []

    def start(copy, when=None):
        sends.append((copy, when))
        if when is None:
            copy.start()
        else:
            pl.when(when)(copy.start)

    kinds = (1, 0, 2)
    for kind in kinds:
        for side in range(2):
            z = me_z + 2 * side - 1
            mine = part(me_z, me_x, me_f, kind)
            start(
                remote(mine, mine, own_send.at[side, kind], z_recv.at[me_z, kind], {"sub": z}),
                inside(z),
            )
    own = gathered.at[me_z, 0, pl.ds(pl.multiple_of(me_f * faces, faces), faces), :]
    start(remote(own, own, swap_send.at[0], swap_recv.at[0], {"face": other_f}))
    own = codes.at[me_z, me_f]
    start(remote(own, own, swap_send.at[1], swap_recv.at[1], {"face": other_f}))

    first = me_z * blocks + me_f * half
    load_mortar.wait()
    cell = row_to_column(cell_ref[...].astype(F32), cols).astype(jnp.int32)
    rate = row_to_column(rate_ref[...], cols)
    offset = (
        jnp.broadcast_to(cell, (cols, dofs))
        - lax.broadcasted_iota(jnp.int32, (cols, dofs), 1)
        - first * dofs
    )
    rates = jnp.broadcast_to(rate, (cols, dofs))

    @pl.loop(0, half)
    def _(b):
        term = jnp.where(offset == b * dofs, rates, 0.0)
        pumped[b] = (pumped[b].astype(F32) + term).astype(BF16)

    step = min(16, half)

    def compute(z, opening):
        targets = 2 * (first + lax.broadcasted_iota(jnp.int32, (half, faces), 0))
        picks = []
        for f in range(2):
            code = jnp.broadcast_to(codes[z, f], (half, faces))
            pick = jnp.where(code == targets, 1.0, 0.0) - jnp.where(code == targets + 1, 1.0, 0.0)
            picks.append(pick.astype(BF16))
        weights[...] = jnp.dot(
            jnp.concatenate(picks, axis=1), gathered[z, 0], preferred_element_type=F32
        )

        @pl.loop(0, half // step)
        def _(i):
            rows = []
            for j in range(step):
                b = i * step + j
                rows.append((pumped[b].astype(F32) * weights[pl.ds(b, 1), :]).astype(BF16))
            flux = jnp.dot(
                jnp.concatenate(rows, axis=0), gathered[z, 1], preferred_element_type=F32
            )
            at = pl.ds(pl.multiple_of(i * (step * cols), step * cols), step * cols)
            if not opening:
                flux = flux + total[at, :]
            total[at, :] = flux

    theirs = gathered.at[me_z, 0, pl.ds(pl.multiple_of(other_f * faces, faces), faces), :]
    remote(theirs, theirs, swap_send.at[0], swap_recv.at[0], {"face": other_f}).wait_recv()
    theirs = codes.at[me_z, other_f]
    remote(theirs, theirs, swap_send.at[1], swap_recv.at[1], {"face": other_f}).wait_recv()
    compute(me_z, True)

    def pass_on_z(k):
        z, onward = source(k)
        for kind in kinds:
            mine = part(z, me_x, me_f, kind)
            remote(
                mine, mine, z_send.at[z, kind], z_recv.at[z, kind], {"face": other_f}
            ).wait_recv()
            start(
                remote(mine, mine, z_send.at[z, kind], z_recv.at[z, kind], {"sub": onward}),
                inside(onward),
            )
            if kind < 2:
                for dx in range(1, width):
                    x = lax.rem(me_x + dx, width)
                    start(remote(
                        mine, mine, x_send.at[z, x, kind], x_recv.at[z, me_x, kind], {"rhs": x}
                    ))
            start(remote(
                mine, mine, core_send.at[z, me_x, kind], core_recv.at[z, me_x, kind],
                {"face": other_f},
            ))

    def pass_on_x(k):
        z, _ = source(k)
        for kind in kinds[:2]:
            for dx in range(1, width):
                x = lax.rem(me_x + width - dx, width)
                came = part(z, x, me_f, kind)
                remote(
                    came, came, x_send.at[z, x, kind], x_recv.at[z, x, kind], {"face": other_f}
                ).wait_recv()
                start(remote(
                    came, came, core_send.at[z, x, kind], core_recv.at[z, x, kind],
                    {"face": other_f},
                ))

    def finish(k):
        z, _ = source(k)
        for kind in kinds:
            for dx in range(width if kind < 2 else 1):
                x = lax.rem(me_x + dx, width)
                came = part(z, x, other_f, kind)
                remote(
                    came, came, core_send.at[z, x, kind], core_recv.at[z, x, kind],
                    {"face": other_f},
                ).wait_recv()
        compute(z, False)

    for k in range(1, subs):
        pass_on_z(k)
    for k in range(1, subs):
        pass_on_x(k)
        if k > 1:
            finish(k - 1)
    if subs > 1:
        finish(subs - 1)
    load_projection.wait()
    for copy, when in sends:
        if when is None:
            copy.wait_send()
        else:
            pl.when(when)(copy.wait_send)


def project(summed_ref, projection_ref, out_ref, staged, sems):
    parts, tile, _ = staged.shape
    copies = []
    for i in range(parts):
        at = pl.ds(i * tile, tile)
        staged[i] = jnp.dot(
            summed_ref[at, :].astype(BF16), projection_ref[...], preferred_element_type=F32
        )
        copies.append(pltpu.make_async_copy(staged.at[i], out_ref.at[at], sems.at[i]))
        copies[-1].start()
    for copy in copies:
        copy.wait()


def on_device(
    mortar_in, pump_rate, well_cell, face_owner, face_slot, face_scale, section, basis, projection
):
    blocks, cols, dofs = mortar_in.shape
    faces = face_slot.shape[0]
    subs, width = lax.axis_size("sub"), lax.axis_size("rhs")
    half = blocks // 2
    sizes = (subs, width, faces, blocks, cols, dofs)
    vmem = pl.BlockSpec(memory_space=pltpu.VMEM)
    hbm = pl.BlockSpec(memory_space=pl.ANY)
    dma = pltpu.SemaphoreType.DMA
    summed, projection_near = pl.pallas_call(
        functools.partial(kernel, sizes),
        out_shape=(pltpu.VMEM((half * cols, dofs), F32), pltpu.VMEM((dofs, dofs), BF16)),
        in_specs=[hbm] * 9,
        out_specs=(vmem, vmem),
        scratch_shapes=[
            pltpu.VMEM((1, faces), jnp.int32),
            pltpu.VMEM((1, faces), jnp.int32),
            pltpu.VMEM((1, 1), jnp.int32),
            pltpu.VMEM((1, cols), jnp.int32),
            pltpu.VMEM((1, cols), F32),
            pltpu.VMEM((1, faces), jnp.int32),
            pltpu.VMEM((subs, 2, 2 * faces, dofs), BF16),
            pltpu.VMEM((subs, 2, 1, faces), jnp.int32),
            pltpu.VMEM((half, cols, dofs), BF16),
            pltpu.VMEM((half, dofs), F32),
            dma((9,)),
            dma((2, 3)),
            dma((2,)), dma((2,)),
            dma((subs, 3)), dma((subs, 3)),
            dma((subs, width, 2)), dma((subs, width, 2)),
            dma((subs, width, 3)), dma((subs, width, 3)),
        ],
        compiler_params=pltpu.CompilerParams(collective_id=0, has_side_effects=True),
    )(
        face_owner.reshape(1, faces), face_slot.reshape(1, faces), section.reshape(1, 1),
        well_cell.reshape(1, cols), pump_rate.reshape(1, cols), mortar_in, face_scale, basis,
        projection,
    )
    rows = half * cols
    parts = 8
    result = pl.pallas_call(
        project,
        out_shape=jax.ShapeDtypeStruct((rows, dofs), F32),
        in_specs=[vmem, vmem],
        out_specs=hbm,
        scratch_shapes=[pltpu.VMEM((parts, rows // parts, dofs), F32), dma((parts,))],
    )(
        pltpu.with_memory_space_constraint(summed, pltpu.VMEM),
        pltpu.with_memory_space_constraint(projection_near, pltpu.VMEM),
    )
    return result.reshape(half, cols, dofs)


def solution(mesh):
    in_specs = (
        P(("groups", "sub"), "rhs", None),
        P(("groups", "rhs")),
        P(("groups", "rhs")),
        P(("groups", "sub", "face"), None),
        P(("groups", "sub", "face")),
        P(("groups", "sub", "face"), None),
        P(("groups", "sub")),
        P(("groups", "sub"), None, None),
        P(),
    )
    out_specs = P(("groups", "sub", "face"), "rhs", None)
    return jax.shard_map(
        on_device, mesh=mesh, in_specs=in_specs, out_specs=out_specs, check_vma=False
    )
```

profile of v0, /device:TPU:0, one launch (start us, length us, event | category | flops | bytes accessed | tf_op | source)
XLA Modules:
  0.0 22.2 jit_solution(4755308521873090431)
XLA Ops:
  0.7 20.0 %shard_map.91 = (f32[2048,256]{1,0:T(8,128)S(1)}, bf16[256,256]{1,0:T(8,128)(2,1)S(1)}) custom-call(s32[1,128]{1,0:T(1,128)} %bitcast.7, s32[1,128]{1,0:T(1,128)} %bitcast.8, s32[1,1]{1,0:T(1,128)} %bitcast.6.section_hbm, s32[1,32]{1,0:T(1,128)} %bitcast.9, f32[1,32]{1,0:T(1,128)} %bitcast.10, bf16[128,32,256]{2,1,0:T(8,128)(2,1)} %mortar_ref.1, ...), custom_call_target="tpu_custom_call" | custom-call | tf_op jit(solution)/shard_map/pallas_call | solution.py:266
  20.6 1.6 %shard_map.92 = f32[2048,256]{1,0:T(8,128)} custom-call(f32[2048,256]{1,0:T(8,128)S(1)} %get-tuple-element.7.summed_ref, bf16[256,256]{1,0:T(8,128)(2,1)S(1)} %get-tuple-element.8.projection_ref), custom_call_target="tpu_custom_call" | custom-call | tf_op jit(solution)/shard_map/pallas_call | solution.py:297
where the time goes:
time: 22.4 us; the launch traced here: 22.2 us
  Pallas kernels  21.6 us (96%)
  between operations  0.66 us (3%)
    pallas_call x1, Pallas kernels, on_device(): pl.pallas_call(functools.partial(kernel, sizes), out_shape=(pltpu.VMEM((h...  20 us
    pallas_call x1, Pallas kernels, on_device(): pl.pallas_call(project, out_shape=jax.ShapeDtypeStruct((rows, dofs), F32)...  1.61 us

commit v1 on v0

v1 whole, which is shorter than its diff:
```python
import functools

import jax
import jax.numpy as jnp
from jax import lax
from jax.experimental import pallas as pl
from jax.experimental.pallas import tpu as pltpu
from jax.sharding import PartitionSpec as P

MESH = pl.DeviceIdType.MESH
F32, BF16 = jnp.float32, jnp.bfloat16
BASIS, SCALE, CODE = 0, 1, 2


def row_to_column(row, length):
    rows = lax.broadcasted_iota(jnp.int32, (length, length), 0)
    lanes = lax.broadcasted_iota(jnp.int32, (length, length), 1)
    spread = jnp.broadcast_to(row, (length, length))
    return jnp.sum(jnp.where(rows == lanes, spread, 0.0), axis=1, keepdims=True)


def kernel(
    sizes,
    owner_hbm, slot_hbm, section_hbm, cell_hbm, rate_hbm, mortar_ref, scale_ref, basis_ref,
    projection_ref,
    total, weights, pumped, basis_last, projection_out,
    owner_ref, slot_ref, section_ref, cell_ref, rate_ref,
    scale_in, packed, codes_out, bases, scales, codes,
    local_sems, swap_send, swap_recv,
    z_send, z_recv, x_send, x_recv, core_send, core_recv,
):
    subs, width, faces, blocks, cols, dofs, room = sizes
    me_z, me_x, me_f = lax.axis_index("sub"), lax.axis_index("rhs"), lax.axis_index("face")
    half = blocks // 2
    other_f = 1 - me_f
    shares = (dofs // (2 * width), room // width)

    low = 1 - (2 * me_z) // subs
    margin = low * me_z + (1 - low) * (subs - 1 - me_z)

    def by_distance(k):
        beyond = (k - 2 * margin - 1 + 4 * subs) // (4 * subs)
        side = (1 - beyond) * (2 * (k % 2) - 1) + beyond * (2 * low - 1)
        reach = (1 - beyond) * ((k + 1) // 2) + beyond * (k - margin)
        return me_z + side * reach

    def in_turn(k):
        return (k - 1) + (k - 1 + subs - me_z) // subs

    def part(z, x, f, kind):
        if kind == CODE:
            return codes.at[z, f]
        share = shares[kind]
        at = pl.ds(pl.multiple_of((f * width + x) * share, share), share)
        return (bases if kind == BASIS else scales).at[z, at, :]

    def remote(src, dst, send, recv, device):
        return pltpu.make_async_remote_copy(
            src_ref=src, dst_ref=dst, send_sem=send, recv_sem=recv,
            device_id=device, device_id_type=MESH,
        )

    load_basis = pltpu.make_async_copy(basis_ref.at[0], bases.at[me_z], local_sems.at[0])
    load_scale = pltpu.make_async_copy(scale_ref, scale_in, local_sems.at[1])
    load_mortar = pltpu.make_async_copy(
        mortar_ref.at[pl.ds(me_f * half, half)], pumped, local_sems.at[2]
    )
    load_projection = pltpu.make_async_copy(projection_ref, projection_out, local_sems.at[3])
    small = [
        pltpu.make_async_copy(src, dst, local_sems.at[4 + i])
        for i, (src, dst) in enumerate((
            (owner_hbm, owner_ref), (slot_hbm, slot_ref), (section_hbm, section_ref),
            (cell_hbm, cell_ref), (rate_hbm, rate_ref),
        ))
    ]
    for copy in small[:3]:
        copy.start()
    load_basis.start()
    load_scale.start()
    barrier = pltpu.get_barrier_semaphore()
    pl.semaphore_signal(barrier, inc=1, device_id={"face": other_f}, device_id_type=MESH)
    for dx in range(1, width):
        pl.semaphore_signal(
            barrier, inc=1, device_id={"rhs": lax.rem(me_x + dx, width)}, device_id_type=MESH
        )
    for dz in range(1, subs):
        pl.semaphore_signal(
            barrier, inc=1, device_id={"sub": lax.rem(me_z + dz, subs)}, device_id_type=MESH
        )
    for copy in small[3:]:
        copy.start()
    load_mortar.start()
    load_projection.start()

    for copy in small[:3]:
        copy.wait()
    load_scale.wait()

    owner = owner_ref[...]
    lanes = lax.broadcasted_iota(jnp.int32, (faces, faces), 1)
    rows = lax.broadcasted_iota(jnp.int32, (faces, faces), 0)
    earlier = jnp.where(rows < lanes, 1.0, 0.0).astype(BF16)
    padded = -(-subs // 16) * 16
    named = lax.broadcasted_iota(jnp.int32, (padded, faces), 0) == jnp.broadcast_to(
        owner, (padded, faces)
    )
    named = jnp.where(named, 1.0, 0.0)
    ranks = jnp.dot(named.astype(BF16), earlier, preferred_element_type=F32)
    rank = jnp.sum(named * ranks, axis=0, keepdims=True).astype(jnp.int32)
    sign = (1 - 2 * section_ref[0]).astype(F32)
    place = lax.broadcasted_iota(jnp.int32, (subs * room, faces), 0) == jnp.broadcast_to(
        owner * room + rank, (subs * room, faces)
    )
    packed[...] = jnp.dot(
        jnp.where(place, sign, 0.0).astype(BF16), scale_in[...], preferred_element_type=F32
    ).astype(BF16)
    spot = lax.broadcasted_iota(jnp.int32, (subs * 2 * room, faces), 0) == jnp.broadcast_to(
        (owner * 2 + me_f) * room + rank, (subs * 2 * room, faces)
    )
    slots = jnp.broadcast_to((slot_ref[...] + 1).astype(F32), (16, faces)).astype(BF16)
    coded = lax.dot_general(
        slots, jnp.where(spot, 1.0, 0.0).astype(BF16), (((1,), (1,)), ((), ())),
        preferred_element_type=F32,
    )
    for d in range(subs):
        codes_out[d] = coded[:1, d * 2 * room:(d + 1) * 2 * room]
    load_basis.wait()
    pl.semaphore_wait(barrier, subs + width - 1)

    sends = []

    def start(copy):
        sends.append(copy)
        copy.start()

    for k in reversed(range(1, subs)):
        d = by_distance(k)
        start(remote(
            part(me_z, me_x, me_f, BASIS), part(me_z, me_x, me_f, BASIS),
            z_send.at[k, BASIS], z_recv.at[me_z, BASIS], {"sub": d},
        ))
        share = shares[SCALE]
        mine = packed.at[pl.ds(pl.multiple_of(d * room + me_x * share, share), share), :]
        start(remote(
            mine, part(me_z, me_x, me_f, SCALE),
            z_send.at[k, SCALE], z_recv.at[me_z, SCALE], {"sub": d},
        ))
        start(remote(
            codes_out.at[d], codes.at[me_z, me_f],
            z_send.at[k, CODE], z_recv.at[me_z, CODE], {"sub": d},
        ))
    own_rows = pl.ds(pl.multiple_of(me_z * room, room), room)

    def own_part(f):
        return scales.at[me_z, pl.ds(pl.multiple_of(f * room, room), room), :]

    start(remote(
        packed.at[own_rows, :], own_part(me_f), swap_send.at[0], swap_recv.at[0],
        {"face": other_f},
    ))
    start(remote(
        codes_out.at[me_z], codes.at[me_z, me_f], swap_send.at[1], swap_recv.at[1],
        {"face": other_f},
    ))
    scales[me_z, pl.ds(pl.multiple_of(me_f * room, room), room), :] = packed[own_rows, :]
    codes[me_z, me_f] = codes_out[me_z]

    first = me_z * blocks + me_f * half
    for copy in small[3:]:
        copy.wait()
    load_mortar.wait()
    cell = row_to_column(cell_ref[...].astype(F32), cols).astype(jnp.int32)
    rate = row_to_column(rate_ref[...], cols)
    offset = (
        jnp.broadcast_to(cell, (cols, dofs))
        - lax.broadcasted_iota(jnp.int32, (cols, dofs), 1)
        - first * dofs
    )
    rates = jnp.broadcast_to(rate, (cols, dofs))

    @pl.loop(0, half)
    def _(b):
        term = jnp.where(offset == b * dofs, rates, 0.0)
        pumped[b] = (pumped[b].astype(F32) + term).astype(BF16)

    step = min(16, half)

    def weigh(z):
        code = jnp.broadcast_to(codes[z, 0] + codes[z, 1], (half, 2 * room)).astype(jnp.int32)
        targets = me_f * half + 1 + lax.broadcasted_iota(jnp.int32, (half, 2 * room), 0)
        picks = jnp.where(code == targets, 1.0, 0.0).astype(BF16)
        weights[...] = jnp.dot(picks, scales[z], preferred_element_type=F32)

    def compute(z, opening):
        weigh(z)

        @pl.loop(0, half // step)
        def _(i):
            rows = []
            for j in range(step):
                b = i * step + j
                rows.append((pumped[b].astype(F32) * weights[pl.ds(b, 1), :]).astype(BF16))
            flux = jnp.dot(
                jnp.concatenate(rows, axis=0), bases[z], preferred_element_type=F32
            )
            at = pl.ds(pl.multiple_of(i * (step * cols), step * cols), step * cols)
            if not opening:
                flux = flux + total[at, :]
            total[at, :] = flux

    remote(
        own_part(other_f), own_part(other_f), swap_send.at[0], swap_recv.at[0], {"face": other_f}
    ).wait_recv()
    theirs = codes.at[me_z, other_f]
    remote(theirs, theirs, swap_send.at[1], swap_recv.at[1], {"face": other_f}).wait_recv()
    compute(me_z, True)

    kinds = (BASIS, SCALE, CODE)

    def pass_on_z(k):
        z = in_turn(k)
        for kind in kinds:
            mine = part(z, me_x, me_f, kind)
            remote(
                mine, mine, core_send.at[z, me_x, kind], z_recv.at[z, kind], {"face": other_f}
            ).wait_recv()
            if kind != CODE:
                for dx in range(1, width):
                    x = lax.rem(me_x + dx, width)
                    start(remote(
                        mine, mine, x_send.at[z, x, kind], x_recv.at[z, me_x, kind], {"rhs": x}
                    ))
            start(remote(
                mine, mine, core_send.at[z, me_x, kind], core_recv.at[z, me_x, kind],
                {"face": other_f},
            ))

    def pass_on_x(k):
        z = in_turn(k)
        for kind in kinds[:2]:
            for dx in range(1, width):
                x = lax.rem(me_x + width - dx, width)
                came = part(z, x, me_f, kind)
                remote(
                    came, came, x_send.at[z, x, kind], x_recv.at[z, x, kind], {"face": other_f}
                ).wait_recv()
                start(remote(
                    came, came, core_send.at[z, x, kind], core_recv.at[z, x, kind],
                    {"face": other_f},
                ))

    def arrive(k):
        z = in_turn(k)
        for kind in kinds:
            for dx in range(width if kind != CODE else 1):
                x = lax.rem(me_x + dx, width)
                came = part(z, x, other_f, kind)
                remote(
                    came, came, core_send.at[z, x, kind], core_recv.at[z, x, kind],
                    {"face": other_f},
                ).wait_recv()
        return z

    for k in range(1, subs):
        pass_on_z(k)
    for k in range(1, subs):
        pass_on_x(k)
        if k > 1:
            compute(arrive(k - 1), False)
    last = arrive(subs - 1)
    weigh(last)
    basis_last[...] = bases[last]
    load_projection.wait()
    for copy in sends:
        copy.wait_send()


def project(total, weights, pumped, basis_ref, projection_ref, out_ref, staged, sems):
    parts, tile, _ = staged.shape
    cols = pumped.shape[1]
    step = tile // cols
    copies = []
    for i in range(parts):
        at = pl.ds(i * tile, tile)
        rows = []
        for j in range(step):
            b = i * step + j
            rows.append((pumped[b].astype(F32) * weights[pl.ds(b, 1), :]).astype(BF16))
        summed = total[at, :] + jnp.dot(
            jnp.concatenate(rows, axis=0), basis_ref[...], preferred_element_type=F32
        )
        staged[i] = jnp.dot(
            summed.astype(BF16), projection_ref[...], preferred_element_type=F32
        )
        copies.append(pltpu.make_async_copy(staged.at[i], out_ref.at[at], sems.at[i]))
        copies[-1].start()
    for copy in copies:
        copy.wait()


def on_device(
    mortar_in, pump_rate, well_cell, face_owner, face_slot, face_scale, section, basis, projection
):
    blocks, cols, dofs = mortar_in.shape
    faces = face_slot.shape[0]
    subs, width = lax.axis_size("sub"), lax.axis_size("rhs")
    half = blocks // 2
    cap = min(faces, -(-2 * faces // subs))
    share = -(-cap // (16 * width)) * 16
    room = share * width
    assert subs > 1 and blocks < 256
    sizes = (subs, width, faces, blocks, cols, dofs, room)
    vmem = pl.BlockSpec(memory_space=pltpu.VMEM)
    hbm = pl.BlockSpec(memory_space=pl.ANY)
    dma = pltpu.SemaphoreType.DMA
    kept = pl.pallas_call(
        functools.partial(kernel, sizes),
        out_shape=(
            pltpu.VMEM((half * cols, dofs), F32),
            pltpu.VMEM((half, dofs), F32),
            pltpu.VMEM((half, cols, dofs), BF16),
            pltpu.VMEM((dofs, dofs), BF16),
            pltpu.VMEM((dofs, dofs), BF16),
        ),
        in_specs=[hbm] * 9,
        out_specs=(vmem,) * 5,
        scratch_shapes=[
            pltpu.VMEM((1, faces), jnp.int32),
            pltpu.VMEM((1, faces), jnp.int32),
            pltpu.SMEM((1,), jnp.int32),
            pltpu.VMEM((1, cols), jnp.int32),
            pltpu.VMEM((1, cols), F32),
            pltpu.VMEM((faces, dofs), BF16),
            pltpu.VMEM((subs * room, dofs), BF16),
            pltpu.VMEM((subs, 1, 2 * room), F32),
            pltpu.VMEM((subs, dofs, dofs), BF16),
            pltpu.VMEM((subs, 2 * room, dofs), BF16),
            pltpu.VMEM((subs, 2, 1, 2 * room), F32),
            dma((9,)),
            dma((2,)), dma((2,)),
            dma((subs, 3)), dma((subs, 3)),
            dma((subs, width, 2)), dma((subs, width, 2)),
            dma((subs, width, 3)), dma((subs, width, 3)),
        ],
        compiler_params=pltpu.CompilerParams(collective_id=0, has_side_effects=True),
    )(
        face_owner.reshape(1, faces), face_slot.reshape(1, faces), section,
        well_cell.reshape(1, cols), pump_rate.reshape(1, cols), mortar_in, face_scale, basis,
        projection,
    )
    rows = half * cols
    parts = 8
    result = pl.pallas_call(
        project,
        out_shape=jax.ShapeDtypeStruct((rows, dofs), F32),
        in_specs=[vmem] * 5,
        out_specs=hbm,
        scratch_shapes=[pltpu.VMEM((parts, rows // parts, dofs), F32), dma((parts,))],
    )(*(pltpu.with_memory_space_constraint(a, pltpu.VMEM) for a in kept))
    return result.reshape(half, cols, dofs)


def solution(mesh):
    in_specs = (
        P(("groups", "sub"), "rhs", None),
        P(("groups", "rhs")),
        P(("groups", "rhs")),
        P(("groups", "sub", "face"), None),
        P(("groups", "sub", "face")),
        P(("groups", "sub", "face"), None),
        P(("groups", "sub")),
        P(("groups", "sub"), None, None),
        P(),
    )
    out_specs = P(("groups", "sub", "face"), "rhs", None)
    return jax.shard_map(
        on_device, mesh=mesh, in_specs=in_specs, out_specs=out_specs, check_vma=False
    )
```

time: 22.4 us -> 19 us (0.85)
  Pallas kernels: 21.6 us -> 18.2 us
    pallas_call x1, Pallas kernels: 20 us -> 16.5 us  [on_device(): pl.pallas_call(functools.partial(kernel, sizes), out_shape=(pltpu.VMEM((h...]
where the time goes in v1:
time: 19 us; the launch traced here: 18.9 us
  Pallas kernels  18.2 us (96%)
  between operations  0.66 us (3%)
    pallas_call x1, Pallas kernels, on_device(): pl.pallas_call(functools.partial(kernel, sizes), out_shape=(pltpu.VMEM((h...  16.5 us
    pallas_call x1, Pallas kernels, on_device(): pl.pallas_call(project, out_shape=jax.ShapeDtypeStruct((rows, dofs), F32)...  1.71 us

profile of v1, /device:TPU:0, one launch (start us, length us, event | category | flops | bytes accessed | tf_op | source)
XLA Modules:
  0.0 18.9 jit_solution(17198745554876662619)
XLA Ops:
  0.7 16.5 %shard_map.91 = (f32[2048,256]{1,0:T(8,128)S(1)}, f32[64,256]{1,0:T(8,128)S(1)}, bf16[64,32,256]{2,1,0:T(8,128)(2,1)S(1)}, bf16[256,256]{1,0:T(8,128)(2,1)S(1)}, bf16[256,256]{1,0:T(8,128)(2,1)S(1)}) custom-call(s32[1,128]{1,0:T(1,128)} %bitcast.5, s32[1,128]{1,0:T(1,128)} %bitcast.6, s32[1]{0:T(128)S(6)} %copy.10.section_hbm, s32[1,32]{1,0:T(1,128)} %bitcast.7, ...), custom_call_target="tpu_custom_call" | custom-call | tf_op jit(solution)/shard_map/pallas_call | solution.py:316
  17.1 1.7 %shard_map.92 = f32[2048,256]{1,0:T(8,128)} custom-call(f32[2048,256]{1,0:T(8,128)S(1)} %get-tuple-element.10.total, f32[64,256]{1,0:T(8,128)S(1)} %get-tuple-element.11.weights, bf16[64,32,256]{2,1,0:T(8,128)(2,1)S(1)} %get-tuple-element.12.pumped, bf16[256,256]{1,0:T(8,128)(2,1)S(1)} %get-tuple-element.13.basis_ref, ...), custom_call_target="tpu_custom_call" | custom-call | tf_op jit(solution)/shard_map/pallas_call | solution.py:353

commit v2 on v1

--- a/solution.py
+++ b/solution.py
@@ -26,8 +26,7 @@
     total, weights, pumped, basis_last, projection_out,
     owner_ref, slot_ref, section_ref, cell_ref, rate_ref,
     scale_in, packed, codes_out, bases, scales, codes,
-    local_sems, swap_send, swap_recv,
-    z_send, z_recv, x_send, x_recv, core_send, core_recv,
+    local_sems, sent, swap_sent, swap_recv, z_recv, x_recv, core_recv, go_up, go_down,
 ):
     subs, width, faces, blocks, cols, dofs, room = sizes
     me_z, me_x, me_f = lax.axis_index("sub"), lax.axis_index("rhs"), lax.axis_index("face")
@@ -35,17 +34,14 @@
     other_f = 1 - me_f
     shares = (dofs // (2 * width), room // width)
 
-    low = 1 - (2 * me_z) // subs
-    margin = low * me_z + (1 - low) * (subs - 1 - me_z)
-
-    def by_distance(k):
-        beyond = (k - 2 * margin - 1 + 4 * subs) // (4 * subs)
-        side = (1 - beyond) * (2 * (k % 2) - 1) + beyond * (2 * low - 1)
-        reach = (1 - beyond) * ((k + 1) // 2) + beyond * (k - margin)
-        return me_z + side * reach
+    def inside(z):
+        return jnp.logical_and(z >= 0, z < subs)
 
     def in_turn(k):
         return (k - 1) + (k - 1 + subs - me_z) // subs
+
+    def turn(z, at):
+        return z - (z + subs - 1 - at) // subs
 
     def part(z, x, f, kind):
         if kind == CODE:
@@ -83,15 +79,22 @@
         pl.semaphore_signal(
             barrier, inc=1, device_id={"rhs": lax.rem(me_x + dx, width)}, device_id_type=MESH
         )
-    for dz in range(1, subs):
-        pl.semaphore_signal(
-            barrier, inc=1, device_id={"sub": lax.rem(me_z + dz, subs)}, device_id_type=MESH
-        )
+    for z in (me_z - 1, me_z + 1):
+        @pl.when(inside(z))
+        def _():
+            pl.semaphore_signal(barrier, inc=1, device_id={"sub": z}, device_id_type=MESH)
     for copy in small[3:]:
         copy.start()
     load_mortar.start()
     load_projection.start()
 
+    neighbours = (me_z + subs - 1) // subs + (2 * subs - 2 - me_z) // subs
+    pl.semaphore_wait(barrier, width + neighbours)
+    if subs > 2:
+        @pl.when(jnp.logical_and(me_z >= 1, me_z + 1 < subs))
+        def _():
+            pl.semaphore_signal(go_up.at[0], inc=1, device_id={"sub": me_z - 1}, device_id_type=MESH)
+            pl.semaphore_signal(go_down.at[0], inc=1, device_id={"sub": me_z + 1}, device_id_type=MESH)
     for copy in small[:3]:
         copy.wait()
     load_scale.wait()
@@ -125,43 +128,71 @@
     for d in range(subs):
         codes_out[d] = coded[:1, d * 2 * room:(d + 1) * 2 * room]
     load_basis.wait()
-    pl.semaphore_wait(barrier, subs + width - 1)
-
-    sends = []
 
     def start(copy):
-        sends.append(copy)
         copy.start()
 
-    for k in reversed(range(1, subs)):
-        d = by_distance(k)
+    def tell(semaphores, j, z):
+        pl.semaphore_signal(
+            semaphores.at[j - 2], inc=1, device_id={"sub": z}, device_id_type=MESH
+        )
+
+    def send(d):
+        came = turn(me_z, d)
         start(remote(
             part(me_z, me_x, me_f, BASIS), part(me_z, me_x, me_f, BASIS),
-            z_send.at[k, BASIS], z_recv.at[me_z, BASIS], {"sub": d},
+            sent.at[BASIS], z_recv.at[came, BASIS], {"sub": d},
         ))
         share = shares[SCALE]
         mine = packed.at[pl.ds(pl.multiple_of(d * room + me_x * share, share), share), :]
         start(remote(
-            mine, part(me_z, me_x, me_f, SCALE),
-            z_send.at[k, SCALE], z_recv.at[me_z, SCALE], {"sub": d},
+            mine, part(me_z, me_x, me_f, SCALE), sent.at[SCALE], z_recv.at[came, SCALE],
+            {"sub": d},
         ))
         start(remote(
-            codes_out.at[d], codes.at[me_z, me_f],
-            z_send.at[k, CODE], z_recv.at[me_z, CODE], {"sub": d},
+            codes_out.at[d], codes.at[me_z, me_f], sent.at[CODE], z_recv.at[came, CODE],
+            {"sub": d},
         ))
+
+    for j in range(2, subs):
+        @pl.when(me_z - j >= 0)
+        def _():
+            pl.semaphore_wait(go_down.at[j - 2], 1)
+            if j < subs - 1:
+                @pl.when(me_z + 1 < subs)
+                def _():
+                    tell(go_down, j + 1, me_z + 1)
+    for j in reversed(range(1, subs)):
+        @pl.when(me_z - j >= 0)
+        def _():
+            send(me_z - j)
+    for j in range(1, subs):
+        @pl.when(me_z + j < subs)
+        def _():
+            if j > 1:
+                pl.semaphore_wait(go_up.at[j - 2], 1)
+                if j < subs - 1:
+                    @pl.when(me_z >= 1)
+                    def _():
+                        tell(go_up, j + 1, me_z - 1)
+            send(me_z + j)
     own_rows = pl.ds(pl.multiple_of(me_z * room, room), room)
 
     def own_part(f):
         return scales.at[me_z, pl.ds(pl.multiple_of(f * room, room), room), :]
 
-    start(remote(
-        packed.at[own_rows, :], own_part(me_f), swap_send.at[0], swap_recv.at[0],
-        {"face": other_f},
-    ))
-    start(remote(
-        codes_out.at[me_z], codes.at[me_z, me_f], swap_send.at[1], swap_recv.at[1],
-        {"face": other_f},
-    ))
+    swaps = [
+        remote(
+            packed.at[own_rows, :], own_part(me_f), swap_sent.at[0], swap_recv.at[0],
+            {"face": other_f},
+        ),
+        remote(
+            codes_out.at[me_z], codes.at[me_z, me_f], swap_sent.at[1], swap_recv.at[1],
+            {"face": other_f},
+        ),
+    ]
+    for copy in swaps:
+        copy.start()
     scales[me_z, pl.ds(pl.multiple_of(me_f * room, room), room), :] = packed[own_rows, :]
     codes[me_z, me_f] = codes_out[me_z]
 
@@ -183,7 +214,7 @@
         term = jnp.where(offset == b * dofs, rates, 0.0)
         pumped[b] = (pumped[b].astype(F32) + term).astype(BF16)
 
-    step = min(16, half)
+    step = min(8, half)
 
     def weigh(z):
         code = jnp.broadcast_to(codes[z, 0] + codes[z, 1], (half, 2 * room)).astype(jnp.int32)
@@ -194,8 +225,7 @@
     def compute(z, opening):
         weigh(z)
 
-        @pl.loop(0, half // step)
-        def _(i):
+        def piece(i):
             rows = []
             for j in range(step):
                 b = i * step + j
@@ -203,16 +233,19 @@
             flux = jnp.dot(
                 jnp.concatenate(rows, axis=0), bases[z], preferred_element_type=F32
             )
-            at = pl.ds(pl.multiple_of(i * (step * cols), step * cols), step * cols)
+            at = pl.ds(i * (step * cols), step * cols)
             if not opening:
                 flux = flux + total[at, :]
             total[at, :] = flux
 
+        for i in range(half // step):
+            piece(i)
+
     remote(
-        own_part(other_f), own_part(other_f), swap_send.at[0], swap_recv.at[0], {"face": other_f}
+        own_part(other_f), own_part(other_f), swap_sent.at[0], swap_recv.at[0], {"face": other_f}
     ).wait_recv()
     theirs = codes.at[me_z, other_f]
-    remote(theirs, theirs, swap_send.at[1], swap_recv.at[1], {"face": other_f}).wait_recv()
+    remote(theirs, theirs, swap_sent.at[1], swap_recv.at[1], {"face": other_f}).wait_recv()
     compute(me_z, True)
 
     kinds = (BASIS, SCALE, CODE)
@@ -222,17 +255,16 @@
         for kind in kinds:
             mine = part(z, me_x, me_f, kind)
             remote(
-                mine, mine, core_send.at[z, me_x, kind], z_recv.at[z, kind], {"face": other_f}
+                mine, mine, sent.at[kind], z_recv.at[k - 1, kind], {"face": other_f}
             ).wait_recv()
             if kind != CODE:
                 for dx in range(1, width):
                     x = lax.rem(me_x + dx, width)
                     start(remote(
-                        mine, mine, x_send.at[z, x, kind], x_recv.at[z, me_x, kind], {"rhs": x}
+                        mine, mine, sent.at[kind], x_recv.at[k - 1, dx - 1, kind], {"rhs": x}
                     ))
             start(remote(
-                mine, mine, core_send.at[z, me_x, kind], core_recv.at[z, me_x, kind],
-                {"face": other_f},
+                mine, mine, sent.at[kind], core_recv.at[k - 1, kind], {"face": other_f}
             ))
 
     def pass_on_x(k):
@@ -242,23 +274,24 @@
                 x = lax.rem(me_x + width - dx, width)
                 came = part(z, x, me_f, kind)
                 remote(
-                    came, came, x_send.at[z, x, kind], x_recv.at[z, x, kind], {"face": other_f}
+                    came, came, sent.at[kind], x_recv.at[k - 1, dx - 1, kind], {"face": other_f}
                 ).wait_recv()
                 start(remote(
-                    came, came, core_send.at[z, x, kind], core_recv.at[z, x, kind],
-                    {"face": other_f},
+                    came, came, sent.at[kind], core_recv.at[k - 1, kind], {"face": other_f}
                 ))
 
     def arrive(k):
         z = in_turn(k)
         for kind in kinds:
-            for dx in range(width if kind != CODE else 1):
-                x = lax.rem(me_x + dx, width)
-                came = part(z, x, other_f, kind)
-                remote(
-                    came, came, core_send.at[z, x, kind], core_recv.at[z, x, kind],
-                    {"face": other_f},
-                ).wait_recv()
+            if kind == CODE:
+                came = codes.at[z, other_f]
+            else:
+                rows = shares[kind] * width
+                at = pl.ds(pl.multiple_of(other_f * rows, rows), rows)
+                came = (bases if kind == BASIS else scales).at[z, at, :]
+            remote(
+                came, came, sent.at[kind], core_recv.at[k - 1, kind], {"face": other_f}
+            ).wait_recv()
         return z
 
     for k in range(1, subs):
@@ -266,13 +299,19 @@
     for k in range(1, subs):
         pass_on_x(k)
         if k > 1:
-            compute(arrive(k - 1), False)
+            z = arrive(k - 1)
+            compute(z, False)
     last = arrive(subs - 1)
     weigh(last)
     basis_last[...] = bases[last]
     load_projection.wait()
-    for copy in sends:
+    for copy in swaps:
         copy.wait_send()
+    for kind, whole in ((BASIS, bases), (SCALE, scales), (CODE, codes)):
+        whole = whole.at[pl.ds(0, subs - 1)]
+        remote(
+            whole, whole, sent.at[kind], core_recv.at[0, kind], {"face": other_f}
+        ).wait_send()
 
 
 def project(total, weights, pumped, basis_ref, projection_ref, out_ref, staged, sems):
@@ -336,11 +375,10 @@
             pltpu.VMEM((subs, dofs, dofs), BF16),
             pltpu.VMEM((subs, 2 * room, dofs), BF16),
             pltpu.VMEM((subs, 2, 1, 2 * room), F32),
-            dma((9,)),
-            dma((2,)), dma((2,)),
-            dma((subs, 3)), dma((subs, 3)),
-            dma((subs, width, 2)), dma((subs, width, 2)),
-            dma((subs, width, 3)), dma((subs, width, 3)),
+            dma((9,)), dma((3,)), dma((2,)), dma((2,)),
+            dma((subs - 1, 3)), dma((subs - 1, max(width - 1, 1), 2)), dma((subs - 1, 3)),
+            pltpu.SemaphoreType.REGULAR((max(subs - 2, 1),)),
+            pltpu.SemaphoreType.REGULAR((max(subs - 2, 1),)),
         ],
         compiler_params=pltpu.CompilerParams(collective_id=0, has_side_effects=True),
     )(

time: 19 us -> 17.2 us (0.905)
  Pallas kernels: 18.2 us -> 16.4 us
    pallas_call x1, Pallas kernels: 16.5 us -> 14.7 us  [on_device(): pl.pallas_call(functools.partial(kernel, sizes), out_shape=(pltpu.VMEM((h...]
where the time goes in v2:
time: 17.2 us; the launch traced here: 17 us
  Pallas kernels  16.4 us (95%)
  between operations  0.66 us (4%)
    pallas_call x1, Pallas kernels, on_device(): pl.pallas_call(functools.partial(kernel, sizes), out_shape=(pltpu.VMEM((h...  14.7 us
    pallas_call x1, Pallas kernels, on_device(): pl.pallas_call(project, out_shape=jax.ShapeDtypeStruct((rows, dofs), F32)...  1.71 us

profile of v2, /device:TPU:0, one launch (start us, length us, event | category | flops | bytes accessed | tf_op | source)
XLA Modules:
  0.0 17.0 jit_solution(12606608894727767531)
XLA Ops:
  0.7 14.7 %shard_map.91 = (f32[2048,256]{1,0:T(8,128)S(1)}, f32[64,256]{1,0:T(8,128)S(1)}, bf16[64,32,256]{2,1,0:T(8,128)(2,1)S(1)}, bf16[256,256]{1,0:T(8,128)(2,1)S(1)}, bf16[256,256]{1,0:T(8,128)(2,1)S(1)}) custom-call(s32[1,128]{1,0:T(1,128)} %bitcast.5, s32[1,128]{1,0:T(1,128)} %bitcast.6, s32[1]{0:T(128)S(6)} %copy.10.section_hbm, s32[1,32]{1,0:T(1,128)} %bitcast.7, ...), custom_call_target="tpu_custom_call" | custom-call | tf_op jit(solution)/shard_map/pallas_call | solution.py:355
  15.3 1.7 %shard_map.92 = f32[2048,256]{1,0:T(8,128)} custom-call(f32[2048,256]{1,0:T(8,128)S(1)} %get-tuple-element.10.total, f32[64,256]{1,0:T(8,128)S(1)} %get-tuple-element.11.weights, bf16[64,32,256]{2,1,0:T(8,128)(2,1)S(1)} %get-tuple-element.12.pumped, bf16[256,256]{1,0:T(8,128)(2,1)S(1)} %get-tuple-element.13.basis_ref, ...), custom_call_target="tpu_custom_call" | custom-call | tf_op jit(solution)/shard_map/pallas_call | solution.py:391
